TPU v7x, 32 devices: a whole 2x2x4 slice. The times are simulated.
32 devices in a mesh: bond: 16 (over z, y, x), op: 2 (over core).
Axes of the slice: x: 2, y: 2, z: 4, core: 2. Of those that a mesh axis runs over, the one named last changes fastest.
Arguments:
- wavefunction: float32 [6, 256, 8192], P(None, None, 'bond'), may hold values from -6 to 6
- left_tiles: bfloat16 [16, 16, 2, 128, 128], P('op', None, None, 'bond'), may hold values from -0.375 to 0.375
- right_tiles: bfloat16 [16, 16, 2, 128, 128], P('op', None, None, 'bond'), may hold values from -0.375 to 0.375
- site_operators: float32 [16, 4, 4], P('op'), may hold values from -1.75 to 1.75
- left_charge: int32 [16], replicated, may hold values from 0 to 7, as said below
- right_charge: int32 [16], replicated, may hold values from 0 to 7, as said below
- channel_charge: int32 [16, 2], replicated, may hold values from -1 to 7, as said below
Outputs:
- sigma_one: float32 [6, 256, 8192], P(None, 'bond', 'op')
- sigma_two: float32 [6, 256, 8192], P(None, 'op', 'bond')
Inputs may be any that keep to these rules, and one draw needn't show every extreme that they name: `left_charge`: each charge labels exactly 2 of the left blocks. `right_charge`: each charge labels exactly 2 of the right blocks. `channel_charge`: column 0 is a left charge shift, each of 0 to 7 used by exactly 2 channels; column 1 is a site charge shift, each of -1, 0 and 1 used by 5 or 6 channels.
All inputs are finite; a program needn't handle non-finite values.
Results may differ from a plain program's by a relative error of at most 0.0057.
Values may be sent and summed in bfloat16 or wider, within the bound.
A program may use at most 128 MiB of HBM per device.

v0:
```python
import jax
import jax.numpy as jnp
from jax import lax
from jax.sharding import PartitionSpec as P

M = 2048
B = 128
NQ = 8
DP = 4
NB = 16
NPB = 2
site_charge_table = (0, 1, 1, 2)


def block_sources(charge, offset):
    ordering = jnp.argsort(charge, stable=True)
    target = (charge - offset) % NQ
    slot_index = target[:, None] * NPB + jnp.arange(NPB, dtype=jnp.int32)[None, :]
    return ordering[slot_index]


def site_masks(site_operators, channel_charge):
    site_charge = jnp.array(site_charge_table, dtype=jnp.int32)
    charge_step = site_charge[:, None] - site_charge[None, :]
    allowed = (charge_step[None, :, :] - channel_charge[:, 1][:, None, None]) % NQ == 0
    return jnp.where(allowed, site_operators, jnp.zeros_like(site_operators))


def pick_left(tile_full, left_order, row_class):
    slots = row_class[:, :, None] * NPB + jnp.arange(NPB, dtype=jnp.int32)[None, None, :]
    chosen = left_order[slots]

    def choose_tiles(channel_tiles, channel_rows):
        return channel_tiles[channel_rows]

    return jax.vmap(choose_tiles)(tile_full, chosen)


def right_terms(tile_piece, picked, site_matrix):
    inner_sum = jnp.einsum(
        "cjnab,ckrpjnb->ckrpja", tile_piece, picked, preferred_element_type=jnp.float32
    )
    return jnp.einsum("cpq,ckrqja->ckrpja", site_matrix, inner_sum, precision=lax.Precision.HIGHEST)


def local(
    wavefunction, left_tiles, right_tiles, site_operators, left_charge, right_charge, channel_charge
):
    bond_count = lax.axis_size("bond")
    operator_count = lax.axis_size("op")
    root_count, sector_rows, column_strip = wavefunction.shape
    local_channels = site_operators.shape[0]
    band_rows = sector_rows // bond_count
    first_channel = lax.axis_index("op") * local_channels
    own_charge = lax.dynamic_slice_in_dim(channel_charge, first_channel, local_channels, 0)
    group_width = min(column_strip, B)
    group_count = column_strip // group_width
    site_charge = jnp.array(site_charge_table, dtype=jnp.int32)
    starts = (
        lax.axis_index("bond") * column_strip
        + jnp.arange(group_count, dtype=jnp.int32) * group_width
    )
    classes = (site_charge[starts // M] + right_charge[starts % M // B]) % NQ
    left_order = jnp.argsort(left_charge, stable=True)
    first_class = (own_charge[:, 0][:, None] - classes[None, :]) % NQ
    second_class = jnp.broadcast_to((-classes % NQ)[None, :], first_class.shape)
    right_sources = jax.vmap(block_sources, in_axes=(None, 0))(
        right_charge, -(own_charge[:, 0] + own_charge[:, 1])
    )
    site_matrix = site_masks(site_operators, own_charge)
    sector_psi = wavefunction.astype(jnp.bfloat16).reshape(
        root_count, NPB, B, group_count, group_width
    )
    left_full, right_full = (
        lax.all_gather(left_tiles, "bond", axis=3, tiled=True),
        lax.all_gather(right_tiles, "bond", axis=3, tiled=True),
    )
    first_tiles = pick_left(left_full, left_order, first_class)
    left_side = jnp.einsum(
        "cgmnab,knbgw->ckmagw", first_tiles, sector_psi, preferred_element_type=jnp.float32
    )
    left_side = left_side.astype(jnp.bfloat16).reshape(
        local_channels * root_count, sector_rows, column_strip
    )
    by_rows = lax.all_to_all(left_side, "bond", split_axis=1, concat_axis=2, tiled=True)
    by_rows = by_rows.reshape(local_channels, root_count, band_rows, DP, NB, B)

    def pick_columns(channel_rows, source_index):
        return channel_rows[:, :, :, source_index]

    picked_rows = jax.vmap(pick_columns)(by_rows, right_sources)
    partial_one = right_terms(right_full, picked_rows, site_matrix).sum(axis=0)
    partial_one = partial_one.reshape(root_count, band_rows, DP * M)
    share_width = DP * M // operator_count
    summed = lax.psum(partial_one, "op")
    sigma_one = lax.dynamic_slice_in_dim(summed, lax.axis_index("op") * share_width, share_width, 2)
    rounded_one = summed.astype(jnp.bfloat16)
    rounded_blocks = rounded_one.reshape(root_count, band_rows, DP, NB, B)

    def pick_shared_columns(source_index):
        return rounded_blocks[:, :, :, source_index]

    picked_again = jax.vmap(pick_shared_columns)(right_sources)
    right_side = right_terms(right_full, picked_again, site_matrix)
    right_side = right_side.astype(jnp.bfloat16).reshape(
        local_channels * root_count, band_rows, DP * M
    )
    by_columns = lax.all_to_all(right_side, "bond", split_axis=2, concat_axis=1, tiled=True)
    by_columns = by_columns.reshape(local_channels, root_count, NPB, B, group_count, group_width)
    second_tiles = pick_left(left_full, left_order, second_class)
    partial_two = jnp.einsum(
        "cgmnab,cknbgw->ckmagw", second_tiles, by_columns, preferred_element_type=jnp.float32
    ).sum(axis=0)
    partial_two = partial_two.reshape(root_count, sector_rows, column_strip)
    sigma_two = lax.psum_scatter(partial_two, "op", scatter_dimension=1, tiled=True)
    return (sigma_one, sigma_two)


def solution(mesh):
    return jax.shard_map(
        local,
        mesh=mesh,
        in_specs=(
            P(None, None, "bond"),
            P("op", None, None, "bond", None),
            P("op", None, None, "bond", None),
            P("op", None, None),
            P(),
            P(),
            P(),
        ),
        out_specs=(P(None, "bond", "op"), P(None, "op", "bond")),
        check_vma=False,
    )
```

profile of v0, /device:TPU:0, one launch (start us, length us, event | category | flops | bytes accessed | tf_op | source)
XLA Modules:
  0.0 1423.8 jit_solution(16086372687354315001)
XLA Ops:
  16.9 138.4 %all-gather.3.cloned.1.call-done = bf16[8,16,2,128,128]{4,3,2,1,0:T(8,128)(2,1)} async-done(((bf16[8,16,2,8,128]{4,3,2,1,0:T(8,128)(2,1)}), bf16[8,16,2,128,128]{4,3,2,1,0:T(8,128)(2,1)}) %all-gather.3.cloned.1.call-update) | async-done | bytes 8388624 | tf_op jit(solution)/shard_map/all_gather | solution.py:75
  168.6 32.3 %copy.103 = bf16[8,6,2,128,4,128]{5,4,1,0,3,2:T(4,128)(2,1)} copy(bf16[8,6,2,128,4,128]{5,3,1,2,0,4:T(8,128)(2,1)S(1)} %fusion.10) | data formatting | bytes 25165824 | tf_op jit(solution)/shard_map/reshape | solution.py:82
  201.0 19.0 %reshape.505 = bf16[48,256,512]{2,0,1:T(8,128)(2,1)} reshape(bf16[8,6,2,128,4,128]{5,4,1,0,3,2:T(4,128)(2,1)} %copy.103) | data formatting | bytes 25165824 | tf_op jit(solution)/shard_map/reshape | solution.py:82
  230.0 272.9 %all-to-all-done = bf16[48,256,512]{2,0,1:T(8,128)(2,1)} async-done(((bf16[48,256,512]{2,0,1:T(8,128)(2,1)}), bf16[48,256,512]{2,0,1:T(8,128)(2,1)}, u32[]{:S(2)}, u32[]{:S(2)}) %all-to-all-start) | async-done | bytes 12582944 | tf_op jit(solution)/shard_map/all_to_all | solution.py:85
  502.9 14.4 %copy.149 = bf16[48,16,16,512]{3,1,2,0:T(8,128)(2,1)} copy(bf16[48,16,16,512]{3,0,2,1:T(8,128)(2,1)} %bitcast.9) | data formatting | bytes 25165824 | tf_op jit(solution)/shard_map/all_to_all | solution.py:85
  517.4 20.3 %reshape.414 = bf16[8,6,16,4,16,128]{5,4,3,2,1,0:T(8,128)(2,1)} reshape(bf16[48,16,16,512]{3,2,1,0:T(8,128)(2,1)} %bitcast.117) | data formatting | bytes 25165824 | tf_op jit(solution)/shard_map/reshape | solution.py:86
  537.6 25.7 %copy.72 = bf16[8,6,16,4,16,128]{5,2,4,3,1,0:T(8,128)(2,1)} copy(bf16[8,6,16,4,16,128]{5,4,3,2,1,0:T(8,128)(2,1)} %reshape.414) | data formatting | bytes 25165824 | tf_op jit(solution)/shard_map/reshape | solution.py:86
  563.4 19.4 %gather_fusion.7 = bf16[256,6,16,4,128]{4,2,3,1,0:T(8,128)(2,1)} fusion(bf16[8,6,16,4,16,128]{5,2,4,3,1,0:T(8,128)(2,1)} %copy.72, s32[256]{0:T(256)S(1)} %reshape.474), kind=kCustom, calls=%fused_computation.7 | custom fusion | bytes 50333696 | tf_op jit(solution)/shard_map/vmap()/gather | solution.py:89
  588.7 23.5 %fusion.15 = f32[8,6,16,4,16,128]{5,2,3,1,4,0:T(8,128)} fusion(bf16[8,16,2,6,16,4,128]{6,4,5,3,2,1,0:T(8,128)(2,1)} %bitcast.115, bf16[8,16,2,128,128]{4,3,2,1,0:T(8,128)(2,1)} %all-gather.5.cloned.1.call-done), kind=kOutput, calls=%fused_computation.25 | convolution fusion | flops 3221225472 | bytes 58720256 | tf_op jit(solution)/shard_map/cjnab,ckrpjnb->ckrpja/dot_general | solution.py:40
  612.3 32.9 %fusion.25 = f32[6,16,4,16,128]{4,2,3,1,0:T(4,128)S(1)} fusion(f32[8,6,16,4,16,128]{5,2,3,1,4,0:T(8,128)} %fusion.15, f32[8,4,4,1,1,1]{0,2,1,5,4,3:T(4,128)S(1)} %select_bitcast_fusion), kind=kOutput, calls=%fused_computation.31 | convolution fusion | flops 301989888 | bytes 28312064 | tf_op jit(solution)/shard_map/cpq,ckrqja->ckrpja/dot_general | solution.py:43
  648.2 131.5 %all-reduce.2.cloned.1.call-done = f32[6,16,8192]{2,1,0:T(8,128)} async-done(((f32[6,16,8192]{2,1,0:T(8,128)}), f32[6,16,8192]{2,1,0:T(8,128)}) %all-reduce.2.cloned.1.call-update) | async-done | bytes 3145744 | tf_op jit(solution)/shard_map/psum | solution.py:95
  783.2 13.6 gather_fusion.4
  796.8 23.5 %fusion.18 = f32[8,6,16,4,16,128]{5,2,3,1,4,0:T(8,128)} fusion(bf16[8,16,2,6,16,4,128]{6,4,5,3,2,1,0:T(8,128)(2,1)} %bitcast.116, bf16[8,16,2,128,128]{4,3,2,1,0:T(8,128)(2,1)} %all-gather.5.cloned.1.call-done), kind=kOutput, calls=%fused_computation.26 | convolution fusion | flops 3221225472 | bytes 58720256 | tf_op jit(solution)/shard_map/cjnab,ckrpjnb->ckrpja/dot_general | solution.py:40
  820.4 56.9 %convert_bitcast_fusion = bf16[8,6,16,4,16,128]{5,3,4,2,1,0:T(4,128)(2,1)S(1)} fusion(f32[8,4,4,1,1,1]{2,1,5,4,3,0:T(4,128)S(1)} %copy.95, f32[8,6,16,4,16,128]{5,2,3,1,4,0:T(8,128)} %fusion.18), kind=kOutput, calls=%fused_computation.24 | convolution fusion | flops 308281344 | bytes 37749248 | tf_op jit(solution)/shard_map/cpq,ckrqja->ckrpja/dot_general | solution.py:43
  883.8 19.3 %reshape.417 = bf16[48,16,8192]{2,1,0:T(8,128)(2,1)} reshape(bf16[8,6,16,4,16,128]{5,4,3,2,1,0:T(8,128)(2,1)} %copy.81) | data formatting | bytes 25165824 | tf_op jit(solution)/shard_map/reshape | solution.py:105
  903.1 47.8 %copy.82 = bf16[48,16,8192]{0,1,2:T(8,128)(2,1)} copy(bf16[48,16,8192]{2,1,0:T(8,128)(2,1)} %reshape.417) | data formatting | bytes 25165824 | tf_op jit(solution)/shard_map/reshape | solution.py:105
  950.9 51.9 %reshape.506 = bf16[16,2,196608]{2,1,0:T(2,128)(2,1)} reshape(bf16[8192,16,48]{2,1,0:T(8,128)(2,1)} %bitcast.113) | data formatting | bytes 25165824
  1002.8 7.0 all-to-all-start.1
  1017.6 229.6 %all-to-all-done.1 = bf16[16,2,196608]{2,1,0:T(2,128)(2,1)} async-done(((bf16[16,2,196608]{2,1,0:T(2,128)(2,1)}), bf16[16,2,196608]{2,1,0:T(2,128)(2,1)}, u32[]{:S(2)}, u32[]{:S(2)}) %all-to-all-start.1) | async-done | bytes 12582944 | tf_op jit(solution)/shard_map/all_to_all | solution.py:108
  1247.2 33.6 %reshape.507 = bf16[8192,16,48]{2,1,0:T(8,128)(2,1)} reshape(bf16[16,2,196608]{2,1,0:T(2,128)(2,1)} %all-to-all-done.1) | data formatting | bytes 25165824
  1280.8 40.1 %copy.83 = bf16[48,16,16,512]{3,1,2,0:T(8,128)(2,1)} copy(bf16[48,16,16,512]{0,1,3,2:T(8,128)(2,1)} %bitcast.114) | data formatting | bytes 25165824 | tf_op jit(solution)/shard_map/all_to_all | solution.py:108
  1320.8 18.2 %reshape.418 = bf16[8,6,2,128,4,128]{5,4,3,2,1,0:T(4,128)(2,1)} reshape(bf16[48,16,16,512]{3,2,1,0:T(8,128)(2,1)} %bitcast.118) | data formatting | bytes 25165824 | tf_op jit(solution)/shard_map/reshape | solution.py:109
  1339.0 11.7 fusion.28
  1359.4 57.6 %reduce-scatter.2.cloned.1.call-done = f32[6,128,512]{2,1,0:T(8,128)} async-done(((f32[6,256,512]{2,1,0:T(8,128)}), f32[6,128,512]{2,1,0:T(8,128)}) %reduce-scatter.2.cloned.1.call-update) | async-done | bytes 1572880 | tf_op jit(solution)/shard_map/reduce_scatter | solution.py:115
  (82 shorter events, 68.4 us)
Async XLA Ops:
  7.2 3.4 copy-start
  7.2 148.1 %all-gather.3.cloned.1.call-start = ((), (), s32[]{:S(2)}) async-start(), calls=%async_computation.3 | async-start | bytes 8912896 | tf_op jit(solution)/shard_map/all_gather | solution.py:75
  13.3 148.3 %copy-start.2 = (s32[16]{0:T(128)}, s32[16]{0:T(128)S(1)}, u32[]{:S(2)}) copy-start(s32[16]{0:T(128)S(1)} %get-tuple-element.4) | copy-start | bytes 196
  220.0 6.1 copy-start.4
  220.0 282.9 %all-to-all-start = ((bf16[48,256,512]{2,0,1:T(8,128)(2,1)}), bf16[48,256,512]{2,0,1:T(8,128)(2,1)}, u32[]{:S(2)}, u32[]{:S(2)}) async-start(bf16[48,256,512]{2,0,1:T(8,128)(2,1)} %reshape.505), calls=%async_computation | async-start | bytes 25165824 | tf_op jit(solution)/shard_map/all_to_all | solution.py:85
  225.0 363.7 %all-gather.5.cloned.1.call-start = ((), (), s32[]{:S(2)}) async-start(), calls=%async_computation.4 | async-start | bytes 8912896 | tf_op jit(solution)/shard_map/all_gather | solution.py:76
  225.8 553.9 %all-reduce.2.cloned.1.call-start = ((), (), s32[]{:S(2)}) async-start(), calls=%async_computation.5 | async-start | bytes 6291456 | tf_op jit(solution)/shard_map/psum | solution.py:95
  227.6 2.2 copy-start.5
  227.6 2.2 copy-start.8
  227.6 2.3 copy-start.6
  1002.8 7.0 copy-start.7
  1002.8 7.3 copy-start.3
  1002.8 244.3 %all-to-all-start.1 = ((bf16[16,2,196608]{2,1,0:T(2,128)(2,1)}), bf16[16,2,196608]{2,1,0:T(2,128)(2,1)}, u32[]{:S(2)}, u32[]{:S(2)}) async-start(bf16[16,2,196608]{2,1,0:T(2,128)(2,1)} %reshape.506), calls=%async_computation.1 | async-start | bytes 25165824 | tf_op jit(solution)/shard_map/all_to_all | solution.py:108
  1009.8 407.3 %reduce-scatter.2.cloned.1.call-start = ((), (), s32[]{:S(2)}) async-start(), calls=%async_computation.6 | async-start | bytes 4718592 | tf_op jit(solution)/shard_map/reduce_scatter | solution.py:115
  1339.0 78.1 %copy-start.1 = (s32[16,2]{0,1:T(2,128)S(1)}, s32[16,2]{0,1:T(2,128)}, u32[]{:S(2)}) copy-start(s32[16,2]{0,1:T(2,128)} %param.15) | copy-start | bytes 388
Sparse Core Ops, SparseCore 0:
  10.7 144.5 all-gather.2
  228.6 360.1 all-gather.4
  648.1 131.6 all-reduce.1
  1356.9 60.1 reduce-scatter.1
where the time goes:
time: 1430 us; the launch traced here: 1420 us
  waiting for transfers between devices  837 us (59%)
  local copies, waits for them, and re-layouts  396 us (28%)
  matrix products  156 us (11%)
  between operations  14.3 us (1%)
    all_to_all x1, waiting for transfers between devices, local(): lax.all_to_all(left_side, 'bond', split_axis=1, concat_axis=2, tiled=True)  273 us
    all_to_all x1, waiting for transfers between devices, local(): lax.all_to_all(right_side, 'bond', split_axis=2, concat_axis=1, tiled=True)  230 us
    all_gather x1, waiting for transfers between devices, local(): lax.all_gather(left_tiles, 'bond', axis=3, tiled=True)  138 us
    psum x1, waiting for transfers between devices, local(): summed = lax.psum(partial_one, 'op')  132 us
    dot_general x2, matrix products, right_terms(): jnp.einsum('cpq,ckrqja->ckrpja', site_matrix, inner_sum, precision=lax.Pr...  89.8 us
    unnamed x21, local copies, waits for them, and re-layouts  86 us
    reshape x2, local copies, waits for them, and re-layouts, local(): right_side.astype(jnp.bfloat16)  67 us
    reduce_scatter x1, waiting for transfers between devices, local(): lax.psum_scatter(partial_two, 'op', scatter_dimension=1, tiled=True)  57.6 us
  transfers between devices with their start and end apart: 6, of which 6 were waited for; matrix products, arithmetic and copies ran while one was open for 7% of the time, Pallas kernels for 0%

commit v1 on v0

--- a/solution.py
+++ b/solution.py
@@ -10,6 +10,18 @@
 NB = 16
 NPB = 2
 site_charge_table = (0, 1, 1, 2)
+
+
+def collect(array, axis, dim):
+    ways, here = (lax.axis_size(axis), lax.axis_index(axis))
+    grown, reach = (array, 1)
+    while reach < ways:
+        theirs = lax.ppermute(grown, axis, [(d, d ^ reach) for d in range(ways)])
+        mine_first = jnp.concatenate([grown, theirs], axis=dim)
+        theirs_first = jnp.concatenate([theirs, grown], axis=dim)
+        grown = jnp.where(here & reach == 0, mine_first, theirs_first)
+        reach = 2 * reach
+    return grown
 
 
 def block_sources(charge, offset):
@@ -72,7 +84,7 @@
         root_count, NPB, B, group_count, group_width
     )
     left_full, right_full = (
-        lax.all_gather(left_tiles, "bond", axis=3, tiled=True),
+        collect(left_tiles, "bond", 3),
         lax.all_gather(right_tiles, "bond", axis=3, tiled=True),
     )
     first_tiles = pick_left(left_full, left_order, first_class)

time: 1430 us -> 1570 us (1.098)
  waiting for transfers between devices: 837 us -> 947 us
  other arithmetic: 8.51 us -> 28.4 us
    ppermute x0 -> x4, waiting for transfers between devices: none -> 251 us  [collect(): theirs = lax.ppermute(grown, axis, [(d, d ^ reach) for d in range(ways)])]
    all_gather x1 -> x0, waiting for transfers between devices: 138 us -> none  [local(): lax.all_gather(left_tiles, 'bond', axis=3, tiled=True)]
    select_n x0 -> x4, other arithmetic: none -> 20.6 us  [collect(): grown = jnp.where(here & reach == 0, mine_first, theirs_first)]
    unnamed x21 -> x23, local copies, waits for them, and re-layouts: 86 us -> 86 us
  transfers between devices with their start and end apart: 6 -> 9, of which waited for: 6 -> 8; matrix products, arithmetic and copies ran while one was open for 7% -> 6% of each run, Pallas kernels for 0% -> 0%
where the time goes in v1:
time: 1570 us; the launch traced here: 1560 us
  waiting for transfers between devices  947 us (60%)
  local copies, waits for them, and re-layouts  394 us (25%)
  matrix products  156 us (10%)
  other arithmetic  28.4 us (2%)
  starting transfers between devices  22.5 us (1%)
    all_to_all x1, waiting for transfers between devices, local(): lax.all_to_all(left_side, 'bond', split_axis=1, concat_axis=2, tiled=True)  283 us
    ppermute x4, waiting for transfers between devices, collect(): theirs = lax.ppermute(grown, axis, [(d, d ^ reach) for d in range(ways)])  251 us
    all_to_all x1, waiting for transfers between devices, local(): lax.all_to_all(right_side, 'bond', split_axis=2, concat_axis=1, tiled=True)  230 us
    psum x1, waiting for transfers between devices, local(): summed = lax.psum(partial_one, 'op')  125 us
    dot_general x2, matrix products, right_terms(): jnp.einsum('cpq,ckrqja->ckrpja', site_matrix, inner_sum, precision=lax.Pr...  89.8 us
    unnamed x23, local copies, waits for them, and re-layouts  86 us
    reshape x2, local copies, waits for them, and re-layouts, local(): right_side.astype(jnp.bfloat16)  67 us
    reduce_scatter x1, waiting for transfers between devices, local(): lax.psum_scatter(partial_two, 'op', scatter_dimension=1, tiled=True)  57.6 us
  transfers between devices with their start and end apart: 9, of which 8 were waited for; matrix products, arithmetic and copies ran while one was open for 6% of the time, Pallas kernels for 0%

profile of v1, /device:TPU:0, one launch (start us, length us, event | category | flops | bytes accessed | tf_op | source)
XLA Modules:
  0.0 1561.8 jit_solution(17237081784284908915)
XLA Ops:
  25.8 22.7 %collective-permute-done.1 = bf16[8,16,2,16,128]{4,3,2,1,0:T(8,128)(2,1)} collective-permute-done((bf16[8,16,2,16,128]{4,3,2,1,0:T(8,128)(2,1)S(1)}, bf16[8,16,2,16,128]{4,3,2,1,0:T(8,128)(2,1)}, u32[]{:S(2)}, u32[]{:S(2)}) %collective-permute-start.1) | collective-permute-done | bytes 1048608 | tf_op jit(solution)/shard_map/ppermute | solution.py:19
  52.4 44.5 %collective-permute-done.2 = bf16[8,16,2,32,128]{4,3,2,1,0:T(8,128)(2,1)} collective-permute-done((bf16[8,16,2,32,128]{4,3,2,1,0:T(8,128)(2,1)S(1)}, bf16[8,16,2,32,128]{4,3,2,1,0:T(8,128)(2,1)}, u32[]{:S(2)}, u32[]{:S(2)}) %collective-permute-start.2) | collective-permute-done | bytes 2097184 | tf_op jit(solution)/shard_map/ppermute | solution.py:19
  111.3 171.8 %collective-permute-done.3 = bf16[8,16,2,64,128]{4,3,2,1,0:T(8,128)(2,1)} collective-permute-done((bf16[8,16,2,64,128]{4,3,2,1,0:T(8,128)(2,1)}, bf16[8,16,2,64,128]{4,3,2,1,0:T(8,128)(2,1)}, u32[]{:S(2)}, u32[]{:S(2)}) %collective-permute-start.3) | collective-permute-done | bytes 4194336 | tf_op jit(solution)/shard_map/ppermute | solution.py:19
  308.1 32.2 %copy.103 = bf16[8,6,2,128,4,128]{5,4,1,0,3,2:T(4,128)(2,1)} copy(bf16[8,6,2,128,4,128]{5,3,1,2,0,4:T(8,128)(2,1)S(1)} %fusion.10) | data formatting | bytes 25165824 | tf_op jit(solution)/shard_map/reshape | solution.py:94
  340.3 19.0 %reshape.505 = bf16[48,256,512]{2,0,1:T(8,128)(2,1)} reshape(bf16[8,6,2,128,4,128]{5,4,1,0,3,2:T(4,128)(2,1)} %copy.103) | data formatting | bytes 25165824 | tf_op jit(solution)/shard_map/reshape | solution.py:94
  370.7 282.5 %all-to-all-done = bf16[48,256,512]{2,0,1:T(8,128)(2,1)} async-done(((bf16[48,256,512]{2,0,1:T(8,128)(2,1)}), bf16[48,256,512]{2,0,1:T(8,128)(2,1)}, u32[]{:S(2)}, u32[]{:S(2)}) %all-to-all-start) | async-done | bytes 12582944 | tf_op jit(solution)/shard_map/all_to_all | solution.py:97
  653.3 14.4 copy.149
  667.7 20.3 %reshape.414 = bf16[8,6,16,4,16,128]{5,4,3,2,1,0:T(8,128)(2,1)} reshape(bf16[48,16,16,512]{3,2,1,0:T(8,128)(2,1)} %bitcast.117) | data formatting | bytes 25165824 | tf_op jit(solution)/shard_map/reshape | solution.py:98
  688.0 25.7 %copy.72 = bf16[8,6,16,4,16,128]{5,2,4,3,1,0:T(8,128)(2,1)} copy(bf16[8,6,16,4,16,128]{5,4,3,2,1,0:T(8,128)(2,1)} %reshape.414) | data formatting | bytes 25165824 | tf_op jit(solution)/shard_map/reshape | solution.py:98
  713.7 19.3 %gather_fusion.7 = bf16[256,6,16,4,128]{4,2,3,1,0:T(8,128)(2,1)} fusion(bf16[8,6,16,4,16,128]{5,2,4,3,1,0:T(8,128)(2,1)} %copy.72, s32[256]{0:T(256)S(1)} %reshape.474), kind=kCustom, calls=%fused_computation.7 | custom fusion | bytes 50333696 | tf_op jit(solution)/shard_map/vmap()/gather | solution.py:101
  733.1 23.5 %fusion.15 = f32[8,6,16,4,16,128]{5,2,3,1,4,0:T(8,128)} fusion(bf16[8,16,2,6,16,4,128]{6,4,5,3,2,1,0:T(8,128)(2,1)} %bitcast.115, bf16[8,16,2,128,128]{4,3,2,1,0:T(8,128)(2,1)} %all-gather.2.cloned.1.call-done), kind=kOutput, calls=%fused_computation.25 | convolution fusion | flops 3221225472 | bytes 58720256 | tf_op jit(solution)/shard_map/cjnab,ckrpjnb->ckrpja/dot_general | solution.py:52
  756.6 32.7 %fusion.25 = f32[6,16,4,16,128]{4,2,3,1,0:T(4,128)S(1)} fusion(f32[8,6,16,4,16,128]{5,2,3,1,4,0:T(8,128)} %fusion.15, f32[8,4,4,1,1,1]{0,2,1,5,4,3:T(4,128)S(1)} %select_bitcast_fusion), kind=kOutput, calls=%fused_computation.34 | convolution fusion | flops 301989888 | bytes 28312064 | tf_op jit(solution)/shard_map/cpq,ckrqja->ckrpja/dot_general | solution.py:55
  792.3 125.3 %all-reduce.2.cloned.1.call-done = f32[6,16,8192]{2,1,0:T(8,128)} async-done(((f32[6,16,8192]{2,1,0:T(8,128)}), f32[6,16,8192]{2,1,0:T(8,128)}) %all-reduce.2.cloned.1.call-update) | async-done | bytes 3145744 | tf_op jit(solution)/shard_map/psum | solution.py:107
  921.1 13.6 gather_fusion.4
  934.7 23.5 %fusion.18 = f32[8,6,16,4,16,128]{5,2,3,1,4,0:T(8,128)} fusion(bf16[8,16,2,6,16,4,128]{6,4,5,3,2,1,0:T(8,128)(2,1)} %bitcast.116, bf16[8,16,2,128,128]{4,3,2,1,0:T(8,128)(2,1)} %all-gather.2.cloned.1.call-done), kind=kOutput, calls=%fused_computation.26 | convolution fusion | flops 3221225472 | bytes 58720256 | tf_op jit(solution)/shard_map/cjnab,ckrpjnb->ckrpja/dot_general | solution.py:52
  958.2 57.2 %convert_bitcast_fusion = bf16[8,6,16,4,16,128]{5,3,4,2,1,0:T(4,128)(2,1)S(1)} fusion(f32[8,4,4,1,1,1]{2,1,5,4,3,0:T(4,128)S(1)} %copy.95, f32[8,6,16,4,16,128]{5,2,3,1,4,0:T(8,128)} %fusion.18), kind=kOutput, calls=%fused_computation.24 | convolution fusion | flops 308281344 | bytes 37749248 | tf_op jit(solution)/shard_map/cpq,ckrqja->ckrpja/dot_general | solution.py:55
  1021.9 19.3 %reshape.417 = bf16[48,16,8192]{2,1,0:T(8,128)(2,1)} reshape(bf16[8,6,16,4,16,128]{5,4,3,2,1,0:T(8,128)(2,1)} %copy.81) | data formatting | bytes 25165824 | tf_op jit(solution)/shard_map/reshape | solution.py:117
  1041.2 47.8 %copy.82 = bf16[48,16,8192]{0,1,2:T(8,128)(2,1)} copy(bf16[48,16,8192]{2,1,0:T(8,128)(2,1)} %reshape.417) | data formatting | bytes 25165824 | tf_op jit(solution)/shard_map/reshape | solution.py:117
  1088.9 51.9 %reshape.506 = bf16[16,2,196608]{2,1,0:T(2,128)(2,1)} reshape(bf16[8192,16,48]{2,1,0:T(8,128)(2,1)} %bitcast.113) | data formatting | bytes 25165824
  1155.6 229.6 %all-to-all-done.1 = bf16[16,2,196608]{2,1,0:T(2,128)(2,1)} async-done(((bf16[16,2,196608]{2,1,0:T(2,128)(2,1)}), bf16[16,2,196608]{2,1,0:T(2,128)(2,1)}, u32[]{:S(2)}, u32[]{:S(2)}) %all-to-all-start.1) | async-done | bytes 12582944 | tf_op jit(solution)/shard_map/all_to_all | solution.py:120
  1385.2 33.6 %reshape.507 = bf16[8192,16,48]{2,1,0:T(8,128)(2,1)} reshape(bf16[16,2,196608]{2,1,0:T(2,128)(2,1)} %all-to-all-done.1) | data formatting | bytes 25165824
  1418.8 40.1 %copy.83 = bf16[48,16,16,512]{3,1,2,0:T(8,128)(2,1)} copy(bf16[48,16,16,512]{0,1,3,2:T(8,128)(2,1)} %bitcast.114) | data formatting | bytes 25165824 | tf_op jit(solution)/shard_map/all_to_all | solution.py:120
  1458.9 18.2 %reshape.418 = bf16[8,6,2,128,4,128]{5,4,3,2,1,0:T(4,128)(2,1)} reshape(bf16[48,16,16,512]{3,2,1,0:T(8,128)(2,1)} %bitcast.118) | data formatting | bytes 25165824 | tf_op jit(solution)/shard_map/reshape | solution.py:121
  1497.5 57.6 %reduce-scatter.2.cloned.1.call-done = f32[6,128,512]{2,1,0:T(8,128)} async-done(((f32[6,256,512]{2,1,0:T(8,128)}), f32[6,128,512]{2,1,0:T(8,128)}) %reduce-scatter.2.cloned.1.call-update) | async-done | bytes 1572880 | tf_op jit(solution)/shard_map/reduce_scatter | solution.py:127
  (93 shorter events, 121.2 us)
Async XLA Ops:
  7.2 98.4 %copy-start = (s32[16,2]{0,1:T(2,128)S(1)}, s32[16,2]{0,1:T(2,128)}, u32[]{:S(2)}) copy-start(s32[16,2]{0,1:T(2,128)} %param.15) | copy-start | bytes 388
  7.2 97.1 %copy-start.5 = (s32[4]{0:T(128)S(1)}, s32[4]{0:T(128)}, u32[]{:S(2)}) copy-start(s32[4]{0:T(128)} %constant.119.clone) | copy-start | bytes 52
  7.2 97.7 %copy-start.4 = (s32[16]{0:T(128)S(1)}, s32[16]{0:T(128)}, u32[]{:S(2)}) copy-start(s32[16]{0:T(128)} %param.14) | copy-start | bytes 196
  7.2 99.2 %copy-start.9 = (s32[16]{0:T(128)S(1)}, s32[16]{0:T(128)}, u32[]{:S(2)}) copy-start(s32[16]{0:T(128)} %param.13) | copy-start | bytes 196
  7.2 15.2 collective-permute-start
  24.0 24.5 %collective-permute-start.1 = (bf16[8,16,2,16,128]{4,3,2,1,0:T(8,128)(2,1)S(1)}, bf16[8,16,2,16,128]{4,3,2,1,0:T(8,128)(2,1)}, u32[]{:S(2)}, u32[]{:S(2)}) collective-permute-start(bf16[8,16,2,16,128]{4,3,2,1,0:T(8,128)(2,1)S(1)} %maximum_select_fusion.3), channel_id=1, source_target_pairs={{0,4},{2,6},{4,0},{6,2},{8,12},{10,14},{12,8},{14,10},{16,20},{18,... | collective-permute-start | bytes 3145736 | tf_op jit(solution)/shard_map/ppermute | solution.py:19
  50.8 46.1 %collective-permute-start.2 = (bf16[8,16,2,32,128]{4,3,2,1,0:T(8,128)(2,1)S(1)}, bf16[8,16,2,32,128]{4,3,2,1,0:T(8,128)(2,1)}, u32[]{:S(2)}, u32[]{:S(2)}) collective-permute-start(bf16[8,16,2,32,128]{4,3,2,1,0:T(8,128)(2,1)S(1)} %maximum_select_fusion.2), channel_id=1, source_target_pairs={{0,8},{2,10},{4,12},{6,14},{8,0},{10,2},{12,4},{14,6},{16,24},{18,... | collective-permute-start | bytes 6291464 | tf_op jit(solution)/shard_map/ppermute | solution.py:19
  101.9 181.1 %collective-permute-start.3 = (bf16[8,16,2,64,128]{4,3,2,1,0:T(8,128)(2,1)}, bf16[8,16,2,64,128]{4,3,2,1,0:T(8,128)(2,1)}, u32[]{:S(2)}, u32[]{:S(2)}) collective-permute-start(bf16[8,16,2,64,128]{4,3,2,1,0:T(8,128)(2,1)} %maximum_select_fusion.1), channel_id=1, source_target_pairs={{0,16},{2,18},{4,20},{6,22},{8,24},{10,26},{12,28},{14,30},{16,0},... | collective-permute-start | bytes 12582920 | tf_op jit(solution)/shard_map/ppermute | solution.py:19
  107.7 0.8 copy-start.2
  359.3 293.9 %all-to-all-start = ((bf16[48,256,512]{2,0,1:T(8,128)(2,1)}), bf16[48,256,512]{2,0,1:T(8,128)(2,1)}, u32[]{:S(2)}, u32[]{:S(2)}) async-start(bf16[48,256,512]{2,0,1:T(8,128)(2,1)} %reshape.505), calls=%async_computation | async-start | bytes 25165824 | tf_op jit(solution)/shard_map/all_to_all | solution.py:97
  365.5 367.5 %all-gather.2.cloned.1.call-start = ((), (), s32[]{:S(2)}) async-start(), calls=%async_computation.3 | async-start | bytes 8912896 | tf_op jit(solution)/shard_map/all_gather | solution.py:88
  366.3 551.3 %all-reduce.2.cloned.1.call-start = ((), (), s32[]{:S(2)}) async-start(), calls=%async_computation.4 | async-start | bytes 6291456 | tf_op jit(solution)/shard_map/psum | solution.py:107
  368.4 2.2 copy-start.8
  368.4 2.3 copy-start.6
  1140.8 7.0 copy-start.7
  1140.8 7.2 copy-start.3
  1140.8 244.3 %all-to-all-start.1 = ((bf16[16,2,196608]{2,1,0:T(2,128)(2,1)}), bf16[16,2,196608]{2,1,0:T(2,128)(2,1)}, u32[]{:S(2)}, u32[]{:S(2)}) async-start(bf16[16,2,196608]{2,1,0:T(2,128)(2,1)} %reshape.506), calls=%async_computation.1 | async-start | bytes 25165824 | tf_op jit(solution)/shard_map/all_to_all | solution.py:120
  1147.8 407.3 %reduce-scatter.2.cloned.1.call-start = ((), (), s32[]{:S(2)}) async-start(), calls=%async_computation.5 | async-start | bytes 4718592 | tf_op jit(solution)/shard_map/reduce_scatter | solution.py:127
  1477.0 78.0 %copy-start.1 = (s32[16,2]{0,1:T(2,128)S(1)}, s32[16,2]{0,1:T(2,128)}, u32[]{:S(2)}) copy-start(s32[16,2]{0,1:T(2,128)} %param.15) | copy-start | bytes 388
Sparse Core Ops, SparseCore 0:
  369.1 359.4 all-gather.1
  792.1 125.3 all-reduce.1
  1494.9 60.1 reduce-scatter.1
